TPU v7x, 32 devices: a whole 2x2x4 slice. The times are simulated.
32 devices in a mesh: row: 4 (over x, core), col: 8 (over z, y).
Axes of the slice: x: 2, y: 2, z: 4, core: 2. Of those that a mesh axis runs over, the one named last changes fastest.
Arguments:
- trailing: float32 [4096, 4096], P('row', 'col'), may hold values from -6 to 6
- panel_left: float32 [4096, 384], P(('row', 'col')), may hold values from -0.3125 to 0.3125
- panel_right: float32 [8, 1024, 384], P('row', 'col'), may hold values from -1 to 1
- panel_solved: float32 [1024, 1024], P('row', 'col'), may hold values from -1.75 to 1.75
- right_sides: float32 [4096, 1024], P('row', 'col'), may hold values from -6 to 6
- tile_ranks: int32 [8], replicated, may hold values from 64 to 384, as said below
- tile_order: int32 [8], replicated, may hold values from 0 to 7, each once
Outputs:
- trail_new: float32 [4096, 4096], P('row', 'col')
- rhs_new: float32 [4096, 1024], P('row', 'col')
Inputs may be any that keep to these rules, and one draw needn't show every extreme that they name: `tile_ranks`: every rank is a multiple of 64; both 64 and 384 occur in every draw. `tile_order`: each tile appears in exactly one slot.
All inputs are finite; a program needn't handle non-finite values.
Results may differ from a plain program's by a relative error of at most 0.00008.
Values sent between devices are 32-bit elements; how exact they have to be, the bound alone decides.
A program may use at most 64 MiB of HBM per device.

v0:
```python
import jax
import jax.numpy as jnp
from jax import lax
from jax.sharding import PartitionSpec as P


def spread(value, axis, root):
    mine = lax.axis_index(axis) == root
    return lax.psum(jnp.where(mine, value, jnp.zeros_like(value)), axis)


def exact_dot(left, right):
    return jnp.dot(left, right, precision=lax.Precision.HIGHEST, preferred_element_type=jnp.float32)


def on_device(trailing, panel_left, panel_right, panel_solved, right_sides, tile_ranks, tile_order):
    slot_count = panel_right.shape[0]
    tile_count = tile_order.shape[0]
    rank_width = panel_left.shape[1]
    left_rows, right_rows = (
        lax.all_gather(panel_left, "col", axis=0, tiled=True),
        lax.all_gather(panel_right, "col", axis=1, tiled=True),
    )
    tile_rows = left_rows.shape[0] // slot_count
    left_rows = left_rows.reshape(slot_count, tile_rows, rank_width)
    row_index = lax.axis_index("row")
    column = lax.axis_index("col")
    places = jnp.arange(tile_count, dtype=jnp.int32)
    levels = jnp.arange(rank_width, dtype=jnp.int32)
    slot_ids = row_index * slot_count + jnp.arange(slot_count, dtype=jnp.int32)
    my_tiles = jnp.sum(
        jnp.where(places[None, :] == slot_ids[:, None], tile_order[None, :], 0), axis=1
    )
    my_ranks = jnp.sum(
        jnp.where(places[None, :] == my_tiles[:, None], tile_ranks[None, :], 0), axis=1
    )
    keep_mask = (levels[None, :] < my_ranks[:, None]).astype(jnp.float32)
    left_mine = left_rows * keep_mask[:, None, :]
    root_slot = jnp.sum(jnp.where(tile_order == column, places, 0))
    root_row = root_slot // slot_count
    local_slot = root_slot % slot_count
    column_rank = jnp.sum(jnp.where(places == column, tile_ranks, 0))
    column_mask = (levels < column_rank).astype(jnp.float32)
    left_pick = (
        lax.dynamic_index_in_dim(left_rows, local_slot, 0, keepdims=False) * column_mask[None, :]
    )
    right_pick = lax.dynamic_index_in_dim(right_rows, local_slot, 0, keepdims=False)

    def owner_panel():
        return exact_dot(right_pick, left_pick.T)

    def other_panel():
        return jnp.zeros((right_pick.shape[0], tile_rows), jnp.float32)

    column_dense = lax.cond(row_index == root_row, owner_panel, other_panel)
    column_dense = spread(column_dense, "row", root_row)
    solved = jnp.einsum(
        "snk,nj->skj",
        right_rows,
        lax.all_gather(panel_solved, "row", axis=0, tiled=True),
        precision=lax.Precision.HIGHEST,
        preferred_element_type=jnp.float32,
    )
    updates = []
    for slot in range(slot_count):
        left_part = left_mine[slot]
        slot_right_part = right_rows[slot]
        middle = exact_dot(slot_right_part.T, column_dense)
        updates.append(exact_dot(left_part, jnp.concatenate([middle, solved[slot]], 1)))
    update_all = jnp.concatenate(updates, 0)
    trail_new = trailing - update_all[:, :tile_rows]
    rhs_new = right_sides - update_all[:, tile_rows:]
    return (trail_new, rhs_new)


def solution(mesh):
    return jax.shard_map(
        on_device,
        mesh=mesh,
        in_specs=(
            P("row", "col"),
            P(("row", "col"), None),
            P("row", "col", None),
            P("row", "col"),
            P("row", "col"),
            P(),
            P(),
        ),
        out_specs=(P("row", "col"), P("row", "col")),
        check_vma=False,
    )
```

profile of v0, /device:TPU:0, one launch (start us, length us, event | category | flops | bytes accessed | tf_op | source)
XLA Modules:
  0.0 198.6 jit_solution(3108771299947774375)
XLA Ops:
  7.2 0.0 all-gather.3.cloned.1.call-start
  7.2 0.7 all-gather.3.cloned.1.call-update
  7.9 0.0 all-gather.5.cloned.1.call-start
  7.9 0.7 all-gather.5.cloned.1.call-update
  8.6 0.0 all-reduce.2.cloned.1.call-start
  8.7 1.3 fusion.27
  12.6 1.0 copy.10
  13.6 1.3 fusion.28
  14.9 0.6 compare_convert_fusion
  15.6 0.8 fusion.25
  16.4 0.8 fusion.26
  17.2 0.1 compare_convert_fusion.1
  17.3 39.8 %all-gather.3.cloned.1.call-done = f32[1024,384]{1,0:T(8,128)} async-done(((f32[128,384]{1,0:T(8,128)}), f32[1024,384]{1,0:T(8,128)}) %all-gather.3.cloned.1.call-update) | async-done | bytes 1572880 | tf_op jit(solution)/shard_map/all_gather | solution.py:21
  57.1 60.6 %all-gather.5.cloned.1.call-done = f32[2,1024,384]{2,1,0:T(8,128)} async-done(((f32[2,128,384]{2,1,0:T(8,128)}), f32[2,1024,384]{2,1,0:T(8,128)}) %all-gather.5.cloned.1.call-update) | async-done | bytes 3145744 | tf_op jit(solution)/shard_map/all_gather | solution.py:22
  117.7 0.3 conditional.1
  117.7 0.2 broadcast.35
  118.0 1.5 broadcast_select_fusion
  119.5 0.0 all-reduce.2.cloned.1.call-update
  119.5 0.0 copy-start
  119.5 12.9 %all_gather.11 = f32[1024,128]{0,1:T(8,128)S(1)} all-gather(f32[256,128]{0,1:T(8,128)S(1)} %copy.10), channel_id=1, replica_groups=mesh['row'=4,'col'=8] {'row'}, dimensions={0}, use_global_device_ids=true | all-gather | bytes 655360 | tf_op jit(solution)/shard_map/all_gather | solution.py:60
  132.4 2.7 %broadcast_multiply_fusion = f32[2,512,384]{2,1,0:T(8,128)} fusion(f32[2,512,384]{2,1,0:T(8,128)} %bitcast.38, f32[2,384]{1,0:T(2,128)S(1)} %compare_convert_fusion.1), kind=kLoop, calls=%fused_computation.29 | loop fusion | flops 393216 | bytes 3148800 | tf_op jit(solution)/shard_map/mul | solution.py:38
  135.1 0.0 copy-done
  135.1 1.9 fusion.23
  137.1 37.5 %all-reduce.2.cloned.1.call-done = f32[1024,512]{1,0:T(8,128)} async-done(((f32[1024,512]{1,0:T(8,128)}), f32[1024,512]{1,0:T(8,128)}) %all-reduce.2.cloned.1.call-update) | async-done | bytes 2097168 | tf_op jit(solution)/shard_map/psum | solution.py:9
  174.5 0.0 copy-start.2
  174.5 5.2 %fusion.13 = f32[384,512]{0,1:T(8,128)S(1)} fusion(f32[1024,512]{1,0:T(8,128)} %all-reduce.2.cloned.1.call-done, f32[2,1024,384]{2,1,0:T(8,128)S(1)} %copy-done), kind=kOutput, calls=%fused_computation.17 | convolution fusion | flops 2415919104 | bytes 4456448 | tf_op jit(solution)/shard_map/dot_general | solution.py:13
  179.7 0.0 copy-start.1
  179.7 0.0 copy-done.2
  179.7 2.5 %fusion.18 = f32[512,640]{1,0:T(8,128)S(1)} fusion(f32[384,128]{0,1:T(8,128)S(1)} %get-tuple-element.85, f32[384,512]{0,1:T(8,128)S(1)} %fusion.13, f32[2,512,384]{2,1,0:T(8,128)S(1)} %copy-done.2), kind=kOutput, calls=%fused_computation.23 | convolution fusion | flops 1510195200 | bytes 3080192 | tf_op jit(solution)/shard_map/dot_general | solution.py:13
  182.3 0.0 copy-done.1
  182.3 3.8 %fusion.12 = f32[384,512]{0,1:T(8,128)S(1)} fusion(f32[1024,512]{1,0:T(8,128)S(1)} %copy-done.1, f32[2,1024,384]{2,1,0:T(8,128)S(1)} %copy-done), kind=kOutput, calls=%fused_computation.16 | convolution fusion | flops 2415919104 | bytes 4456448 | tf_op jit(solution)/shard_map/dot_general | solution.py:13
  186.1 0.0 copy-start.4
  186.1 2.5 %fusion.14 = f32[512,640]{1,0:T(8,128)S(1)} fusion(f32[384,128]{0,1:T(8,128)S(1)} %get-tuple-element.86, f32[384,512]{0,1:T(8,128)S(1)} %fusion.12, f32[2,512,384]{2,1,0:T(8,128)S(1)} %copy-done.2), kind=kOutput, calls=%fused_computation.19 | convolution fusion | flops 1510195200 | bytes 3080192 | tf_op jit(solution)/shard_map/dot_general | solution.py:13
  188.6 0.0 copy-done.4
  188.6 0.0 copy-start.3
  188.6 0.9 fusion.22
  189.5 0.9 copy-done.3
  190.4 1.6 fusion.9
  (2 shorter events, 0.0 us)
Async XLA Ops:
  7.2 49.9 %all-gather.3.cloned.1.call-start = ((), (), s32[]{:S(2)}) async-start(), calls=%async_computation | async-start | bytes 1769472 | tf_op jit(solution)/shard_map/all_gather | solution.py:21
  7.9 109.8 %all-gather.5.cloned.1.call-start = ((), (), s32[]{:S(2)}) async-start(), calls=%async_computation.1 | async-start | bytes 3538944 | tf_op jit(solution)/shard_map/all_gather | solution.py:22
  8.6 165.9 %all-reduce.2.cloned.1.call-start = ((), (), s32[]{:S(2)}) async-start(), calls=%async_computation.2 | async-start | bytes 4194304 | tf_op jit(solution)/shard_map/psum | solution.py:9
  119.5 15.6 %copy-start = (f32[2,1024,384]{2,1,0:T(8,128)S(1)}, f32[2,1024,384]{2,1,0:T(8,128)}, u32[]{:S(2)}) copy-start(f32[2,1024,384]{2,1,0:T(8,128)} %all-gather.5.cloned.1.call-done) | copy-start | bytes 9437188
  174.5 5.2 %copy-start.2 = (f32[2,512,384]{2,1,0:T(8,128)S(1)}, f32[2,512,384]{2,1,0:T(8,128)}, u32[]{:S(2)}) copy-start(f32[2,512,384]{2,1,0:T(8,128)} %broadcast_multiply_fusion) | copy-start | bytes 4718596
  179.7 2.5 %copy-start.1 = (f32[1024,512]{1,0:T(8,128)S(1)}, f32[1024,512]{1,0:T(8,128)}, u32[]{:S(2)}) copy-start(f32[1024,512]{1,0:T(8,128)} %all-reduce.2.cloned.1.call-done) | copy-start | bytes 6291460
  186.1 2.5 %copy-start.4 = (f32[1024,128]{1,0:T(8,128)S(1)}, f32[1024,128]{1,0:T(8,128)}, u32[]{:S(2)}) copy-start(f32[1024,128]{1,0:T(8,128)} %param.13) | copy-start | bytes 1572868
  188.6 1.8 copy-start.3
Sparse Core Ops, SparseCore 0:
  10.2 46.8 all-gather.2
  59.3 58.3 all-gather.4
  120.6 53.8 all-reduce.1
where the time goes:
time: 199 us
  waiting for transfers between devices  139 us (70%)
  between operations  16.5 us (8%)
  matrix products  15.9 us (8%)
  blocking collectives  12.9 us (6%)
  other arithmetic  11.7 us (6%)
  local copies, waits for them, and re-layouts  2.21 us (1%)
    all_gather x1, waiting for transfers between devices, on_device(): lax.all_gather(panel_right, 'col', axis=1, tiled=True)  60.6 us
    all_gather x1, waiting for transfers between devices, on_device(): lax.all_gather(panel_left, 'col', axis=0, tiled=True)  39.8 us
    psum x1, waiting for transfers between devices, spread(): return lax.psum(jnp.where(mine, value, jnp.zeros_like(value)), axis)  37.5 us
    dot_general x4, matrix products, exact_dot(): jnp.dot(left, right, precision=lax.Precision.HIGHEST, preferred_element_t...  14 us
    all_gather x1, blocking collectives, on_device(): lax.all_gather(panel_solved, 'row', axis=0, tiled=True)  12.9 us
  transfers between devices with their start and end apart: 3, of which 3 were waited for; matrix products, arithmetic and copies ran while one was open for 5% of the time, Pallas kernels for 0%

commit v1 on v0

--- a/solution.py
+++ b/solution.py
@@ -6,7 +6,7 @@
 
 def spread(value, axis, root):
     mine = lax.axis_index(axis) == root
-    return lax.psum(jnp.where(mine, value, jnp.zeros_like(value)), axis)
+    return jnp.sum(lax.all_gather(jnp.where(mine, value, jnp.zeros_like(value)), axis), axis=0)
 
 
 def exact_dot(left, right):

time: 199 us -> 212 us (1.065)
  waiting for transfers between devices: 139 us -> 148 us
  other arithmetic: 11.7 us -> 16.8 us
    all_gather x0 -> x1, waiting for transfers between devices: none -> 43.2 us  [spread(): lax.all_gather(jnp.where(mine, value, jnp.zeros_like(value)), axis)]
    psum x1 -> x0, waiting for transfers between devices: 37.5 us -> none  [spread(): return lax.psum(jnp.where(mine, value, jnp.zeros_like(value)), axis)]
    reduce_sum x0 -> x1, other arithmetic: none -> 5.95 us  [spread(): jnp.sum(lax.all_gather(jnp.where(mine, value, jnp.zeros_like(value)), axi...]
    all_gather x1, waiting for transfers between devices: 39.8 us -> 42.5 us  [on_device(): lax.all_gather(panel_left, 'col', axis=0, tiled=True)]
  transfers between devices with their start and end apart: 3 -> 3, of which waited for: 3 -> 3; matrix products, arithmetic and copies ran while one was open for 5% -> 4% of each run, Pallas kernels for 0% -> 0%
where the time goes in v1:
time: 212 us; the launch traced here: 211 us
  waiting for transfers between devices  148 us (70%)
  other arithmetic  16.8 us (8%)
  between operations  16.5 us (8%)
  matrix products  16 us (8%)
  blocking collectives  12.1 us (6%)
  local copies, waits for them, and re-layouts  2.17 us (1%)
    all_gather x1, waiting for transfers between devices, on_device(): lax.all_gather(panel_right, 'col', axis=1, tiled=True)  60.6 us
    all_gather x1, waiting for transfers between devices, spread(): lax.all_gather(jnp.where(mine, value, jnp.zeros_like(value)), axis)  43.2 us
    all_gather x1, waiting for transfers between devices, on_device(): lax.all_gather(panel_left, 'col', axis=0, tiled=True)  42.5 us
    dot_general x4, matrix products, exact_dot(): jnp.dot(left, right, precision=lax.Precision.HIGHEST, preferred_element_t...  14 us
    all_gather x1, blocking collectives, on_device(): lax.all_gather(panel_solved, 'row', axis=0, tiled=True)  12.1 us
    reduce_sum x1, other arithmetic, spread(): jnp.sum(lax.all_gather(jnp.where(mine, value, jnp.zeros_like(value)), axi...  5.95 us
  transfers between devices with their start and end apart: 3, of which 3 were waited for; matrix products, arithmetic and copies ran while one was open for 4% of the time, Pallas kernels for 0%

profile of v1, /device:TPU:0, one launch (start us, length us, event | category | flops | bytes accessed | tf_op | source)
XLA Modules:
  0.0 211.4 jit_solution(667645683016833403)
XLA Ops:
  7.2 0.0 all-gather.5.cloned.1.call-start
  7.2 0.7 all-gather.5.cloned.1.call-update
  7.9 0.0 all-gather.7.cloned.1.call-start
  7.9 0.7 all-gather.7.cloned.1.call-update
  8.6 0.0 all-gather.9.cloned.1.call-start
  8.7 1.3 fusion.27
  12.6 1.3 fusion.28
  13.9 0.6 compare_convert_fusion
  14.6 42.5 %all-gather.5.cloned.1.call-done = f32[1024,384]{1,0:T(8,128)} async-done(((f32[128,384]{1,0:T(8,128)}), f32[1024,384]{1,0:T(8,128)}) %all-gather.5.cloned.1.call-update) | async-done | bytes 1572880 | tf_op jit(solution)/shard_map/all_gather | solution.py:21
  57.1 60.6 %all-gather.7.cloned.1.call-done = f32[2,1024,384]{2,1,0:T(8,128)} async-done(((f32[2,128,384]{2,1,0:T(8,128)}), f32[2,1024,384]{2,1,0:T(8,128)}) %all-gather.7.cloned.1.call-update) | async-done | bytes 3145744 | tf_op jit(solution)/shard_map/all_gather | solution.py:22
  117.7 0.3 conditional.1
  117.7 0.2 broadcast.35
  118.0 1.5 broadcast_select_fusion
  119.5 0.0 copy-start.5
  119.5 0.0 copy-start.6
  119.5 0.0 copy-start.7
  119.5 0.0 all-gather.9.cloned.1.call-update
  119.5 0.0 copy-start
  119.6 0.9 copy-done.5
  120.4 0.1 copy.10
  120.5 0.0 copy-done.6
  120.5 0.2 fusion.25
  120.7 0.0 copy-done.7
  120.7 0.2 fusion.26
  120.9 12.1 %all_gather.19 = f32[1024,128]{0,1:T(8,128)S(1)} all-gather(f32[256,128]{0,1:T(8,128)S(1)} %copy.10), channel_id=1, replica_groups=mesh['row'=4,'col'=8] {'row'}, dimensions={0}, use_global_device_ids=true | all-gather | bytes 655360 | tf_op jit(solution)/shard_map/all_gather | solution.py:60
  133.1 0.1 compare_convert_fusion.1
  133.1 3.1 %broadcast_multiply_fusion = f32[2,512,384]{2,1,0:T(8,128)} fusion(f32[2,512,384]{2,1,0:T(8,128)} %bitcast.40, f32[2,384]{1,0:T(2,128)S(1)} %compare_convert_fusion.1), kind=kLoop, calls=%fused_computation.29 | loop fusion | flops 393216 | bytes 3148800 | tf_op jit(solution)/shard_map/mul | solution.py:38
  136.3 0.0 copy-done
  136.3 1.9 fusion.23
  138.2 43.2 %all-gather.9.cloned.1.call-done = f32[4096,512]{1,0:T(8,128)} async-done(((f32[1024,512]{1,0:T(8,128)}), f32[4096,512]{1,0:T(8,128)}) %all-gather.9.cloned.1.call-update) | async-done | bytes 8388624 | tf_op jit(solution)/shard_map/all_gather | solution.py:9
  181.4 6.0 %reduce_sum.49 = f32[1024,512]{1,0:T(8,128)} reduce(f32[4,1024,512]{2,1,0:T(8,128)} %bitcast.38, f32[]{:T(128)} %constant.55.clone.1), dimensions={0}, to_apply=%region_6.7 | reduce | flops 1572864 | bytes 10485764 | tf_op jit(solution)/shard_map/reduce_sum | solution.py:9
  187.4 0.0 copy-start.2
  187.4 5.2 %fusion.13 = f32[384,512]{0,1:T(8,128)S(1)} fusion(f32[1024,512]{1,0:T(8,128)} %reduce_sum.49, f32[2,1024,384]{2,1,0:T(8,128)S(1)} %copy-done), kind=kOutput, calls=%fused_computation.17 | convolution fusion | flops 2415919104 | bytes 4456448 | tf_op jit(solution)/shard_map/dot_general | solution.py:13
  192.6 0.0 copy-start.1
  192.6 0.0 copy-done.2
  192.6 2.5 %fusion.18 = f32[512,640]{1,0:T(8,128)S(1)} fusion(f32[384,128]{0,1:T(8,128)S(1)} %get-tuple-element.85, f32[384,512]{0,1:T(8,128)S(1)} %fusion.13, f32[2,512,384]{2,1,0:T(8,128)S(1)} %copy-done.2), kind=kOutput, calls=%fused_computation.23 | convolution fusion | flops 1510195200 | bytes 3080192 | tf_op jit(solution)/shard_map/dot_general | solution.py:13
  195.1 0.0 copy-done.1
  195.1 3.8 %fusion.12 = f32[384,512]{0,1:T(8,128)S(1)} fusion(f32[1024,512]{1,0:T(8,128)S(1)} %copy-done.1, f32[2,1024,384]{2,1,0:T(8,128)S(1)} %copy-done), kind=kOutput, calls=%fused_computation.16 | convolution fusion | flops 2415919104 | bytes 4456448 | tf_op jit(solution)/shard_map/dot_general | solution.py:13
  198.9 0.0 copy-start.4
  198.9 2.5 %fusion.14 = f32[512,640]{1,0:T(8,128)S(1)} fusion(f32[384,128]{0,1:T(8,128)S(1)} %get-tuple-element.86, f32[384,512]{0,1:T(8,128)S(1)} %fusion.12, f32[2,512,384]{2,1,0:T(8,128)S(1)} %copy-done.2), kind=kOutput, calls=%fused_computation.19 | convolution fusion | flops 1510195200 | bytes 3080192 | tf_op jit(solution)/shard_map/dot_general | solution.py:13
  201.5 0.0 copy-done.4
  201.5 0.0 copy-start.3
  201.5 0.9 fusion.22
  202.3 0.9 copy-done.3
  203.3 1.6 fusion.9
  (2 shorter events, 0.0 us)
Async XLA Ops:
  7.2 49.9 %all-gather.5.cloned.1.call-start = ((), (), s32[]{:S(2)}) async-start(), calls=%async_computation | async-start | bytes 1769472 | tf_op jit(solution)/shard_map/all_gather | solution.py:21
  7.9 109.8 %all-gather.7.cloned.1.call-start = ((), (), s32[]{:S(2)}) async-start(), calls=%async_computation.1 | async-start | bytes 3538944 | tf_op jit(solution)/shard_map/all_gather | solution.py:22
  8.6 172.8 %all-gather.9.cloned.1.call-start = ((), (), s32[]{:S(2)}) async-start(), calls=%async_computation.2 | async-start | bytes 10485760 | tf_op jit(solution)/shard_map/all_gather | solution.py:9
  119.5 0.9 copy-start.5
  119.5 1.0 copy-start.6
  119.5 1.2 copy-start.7
  119.5 16.7 %copy-start = (f32[2,1024,384]{2,1,0:T(8,128)S(1)}, f32[2,1024,384]{2,1,0:T(8,128)}, u32[]{:S(2)}) copy-start(f32[2,1024,384]{2,1,0:T(8,128)} %all-gather.7.cloned.1.call-done) | copy-start | bytes 9437188
  187.4 5.2 %copy-start.2 = (f32[2,512,384]{2,1,0:T(8,128)S(1)}, f32[2,512,384]{2,1,0:T(8,128)}, u32[]{:S(2)}) copy-start(f32[2,512,384]{2,1,0:T(8,128)} %broadcast_multiply_fusion) | copy-start | bytes 4718596
  192.6 2.6 %copy-start.1 = (f32[1024,512]{1,0:T(8,128)S(1)}, f32[1024,512]{1,0:T(8,128)}, u32[]{:S(2)}) copy-start(f32[1024,512]{1,0:T(8,128)} %reduce_sum.49) | copy-start | bytes 6291460
  198.9 2.5 %copy-start.4 = (f32[1024,128]{1,0:T(8,128)S(1)}, f32[1024,128]{1,0:T(8,128)}, u32[]{:S(2)}) copy-start(f32[1024,128]{1,0:T(8,128)} %param.13) | copy-start | bytes 1572868
  201.5 1.8 copy-start.3
Sparse Core Ops, SparseCore 0:
  10.2 46.8 all-gather.4
  59.3 58.3 all-gather.6
  119.8 61.5 all-gather.8
